TPU v7x, 256 devices: a whole 4x4x8 slice. The times are simulated.
256 devices in a mesh: blk: 32 (over y_lo, z, core), ffn: 8 (over y_hi, x).
Axes of the slice: x: 4, y: 4 (y_hi: 2, y_lo: 2; y = y_hi * 2 + y_lo), z: 8, core: 2. Of those that a mesh axis runs over, the one named last changes fastest.
Arguments:
- tokens: bfloat16 [8192, 4608], P('blk'), may hold values from -6 to 6
- ln_gain: float32 [4608], replicated, may hold values from 0.5 to 2
- ln_bias: float32 [4608], replicated, may hold values from -3 to 3
- fc1_tiles: bfloat16 [32, 8, 12, 128, 128], P('blk', 'ffn'), may hold values from -0.125 to 0.125
- fc1_index: int32 [32, 8, 12], P('blk', 'ffn'), may hold values from 0 to 647, as said below
- fc1_count: int32 [32, 8], P('blk', 'ffn'), may hold values from 7 to 12, as said below
- fc1_bias: float32 [18432], P('ffn'), may hold values from -3 to 3
- fc2_tiles: bfloat16 [32, 8, 12, 128, 128], P('blk', 'ffn'), may hold values from -0.09375 to 0.09375
- fc2_index: int32 [32, 8, 12], P('blk', 'ffn'), may hold values from 0 to 647, as said below
- fc2_count: int32 [32, 8], P('blk', 'ffn'), may hold values from 7 to 12, as said below
- fc2_bias: float32 [4608], P('ffn'), may hold values from -3 to 3
Outputs:
- result: bfloat16 [8192, 4608], P('blk', 'ffn')
Inputs may be any that keep to these rules, and one draw needn't show every extreme that they name: `fc1_index`: within one index f of ffn, the positions of all live slots (s < the shard's count) are distinct. `fc2_index`: as for fc1_index. `fc1_count`: some shard of every index of ffn has all 12 slots live. `fc2_count`: as for fc1_count.
All inputs are finite; a program needn't handle non-finite values.
Results may differ from a plain program's by a relative error of at most 0.01.
Values may be sent and summed in bfloat16 or wider, within the bound.
A program may use at most 128 MiB of HBM per device.

v0:
```python
import jax
import jax.numpy as jnp
from jax import lax
from jax.sharding import PartitionSpec as P


def add_slots(running_sum, tile_data, slot_pos, live_count, source_blocks, col_blocks):
    tile_width = tile_data.shape[-1]
    slot_total = tile_data.shape[-3]
    tile_list = tile_data.reshape(-1, tile_width, tile_width)
    place_list = slot_pos.reshape(-1).astype(jnp.int32)
    count_list = live_count.reshape(-1).astype(jnp.int32)
    listed = tile_list.shape[0]
    shard_total = listed // slot_total
    alive = (
        jnp.arange(slot_total, dtype=jnp.int32)[None, :] < count_list.reshape(shard_total, 1)
    ).reshape(-1)
    span = min(listed, 48)
    padded = (listed + span - 1) // span * span
    block_ids = jnp.arange(col_blocks, dtype=jnp.int32)

    def one_block(block_no, running):
        start = block_no * span
        tiles_now = lax.dynamic_slice_in_dim(tile_list, start, span, 0)
        places_now = lax.dynamic_slice_in_dim(place_list, start, span, 0)
        alive_now = lax.dynamic_slice_in_dim(alive, start, span, 0)
        tiles_now = jnp.where(alive_now[:, None, None], tiles_now, jnp.zeros_like(tiles_now))
        inputs_now = jnp.take(source_blocks, places_now // col_blocks, axis=0)
        products = jnp.einsum(
            "nti,nij->ntj", inputs_now, tiles_now, preferred_element_type=jnp.float32
        )
        flat_products = products.reshape(span, -1)
        selector = ((places_now % col_blocks)[:, None] == block_ids[None, :]).astype(jnp.float32)
        placed = jnp.einsum("nc,nk->ck", selector, flat_products, precision=lax.Precision.HIGHEST)
        return running + placed

    block_total = padded // span
    return lax.fori_loop(0, block_total, one_block, running_sum)


def on_device(
    tokens,
    ln_gain,
    ln_bias,
    fc1_tiles,
    fc1_index,
    fc1_count,
    fc1_bias,
    fc2_tiles,
    fc2_index,
    fc2_count,
    fc2_bias,
):
    tile_width = fc1_tiles.shape[-1]
    token_rows = tokens.shape[0]
    rows_f = tokens.astype(jnp.float32)
    center = jnp.mean(rows_f, axis=1, keepdims=True)
    spread = jnp.mean((rows_f - center) ** 2, axis=1, keepdims=True)
    normed = ((rows_f - center) / jnp.sqrt(spread + 1e-05) * ln_gain + ln_bias).astype(jnp.bfloat16)
    hidden_cols = fc1_bias.shape[0]
    width = tokens.shape[1]
    first_blocks = hidden_cols // tile_width
    second_blocks = width // tile_width
    normed_blocks = normed.reshape(token_rows, second_blocks, tile_width).transpose(1, 0, 2)
    first_empty = jnp.zeros((first_blocks, token_rows * tile_width), jnp.float32)
    second_empty = jnp.zeros((second_blocks, token_rows * tile_width), jnp.float32)
    bias_blocks = fc1_bias.reshape(first_blocks, 1, tile_width)
    pieces = (
        lax.all_gather(fc1_tiles, "blk", axis=0, tiled=True),
        lax.all_gather(fc1_index, "blk", axis=0, tiled=True),
        lax.all_gather(fc1_count, "blk", axis=0, tiled=True),
    )
    pre_act = add_slots(first_empty, pieces[0], pieces[1], pieces[2], normed_blocks, first_blocks)
    hidden = jnp.maximum(
        pre_act.reshape(first_blocks, token_rows, tile_width) + bias_blocks, 0.0
    ).astype(jnp.bfloat16)
    pieces = (
        lax.all_gather(fc2_tiles, "blk", axis=0, tiled=True),
        lax.all_gather(fc2_index, "blk", axis=0, tiled=True),
        lax.all_gather(fc2_count, "blk", axis=0, tiled=True),
    )
    partial_value = add_slots(second_empty, pieces[0], pieces[1], pieces[2], hidden, second_blocks)
    partial_value = (
        partial_value.reshape(second_blocks, token_rows, tile_width)
        .transpose(1, 0, 2)
        .reshape(token_rows, width)
    )
    branch = lax.psum_scatter(
        partial_value.astype(jnp.bfloat16), "ffn", scatter_dimension=1, tiled=True
    ).astype(jnp.float32)
    share = branch.shape[1]
    own_cols = lax.dynamic_slice_in_dim(rows_f, lax.axis_index("ffn") * share, share, 1)
    return (own_cols + branch + fc2_bias).astype(jnp.bfloat16)


def solution(mesh):
    placed = (
        P("blk", None),
        P(),
        P(),
        P("blk", "ffn", None, None, None),
        P("blk", "ffn", None),
        P("blk", "ffn"),
        P("ffn"),
        P("blk", "ffn", None, None, None),
        P("blk", "ffn", None),
        P("blk", "ffn"),
        P("ffn"),
    )
    return jax.shard_map(
        on_device, mesh=mesh, in_specs=placed, out_specs=P("blk", "ffn"), check_vma=False
    )
```

profile of v0, /device:TPU:2, one launch (start us, length us, event | category | flops | bytes accessed | tf_op | source)
XLA Modules:
  0.0 532.6 jit_solution(2707272190759077825)
XLA Ops:
  23.4 19.9 %all-reduce.2 = (s32[32]{0:T(128)S(1)}, s32[32]{0:T(128)S(1)}) all-reduce(s32[32]{0:T(128)S(1)} %bitcast_dynamic-update-slice_fusion.1, s32[32]{0:T(128)S(1)} %bitcast_dynamic-update-slice_fusion), channel_id=1, replica_groups=mesh['blk'=32,'ffn'=8] {'blk'}, use_global_device_ids=true, to_apply=%add | all-reduce | flops 64 | bytes 512
  43.5 31.4 %all_gather.19 = s32[32,1,12]{2,1,0:T(1,128)S(1)} all-gather(s32[1,1,12]{2,1,0:T(1,128)S(1)} %copy-done.6), channel_id=1, replica_groups=mesh['blk'=32,'ffn'=8] {'blk'}, dimensions={0}, use_global_device_ids=true | all-gather | bytes 1584 | tf_op jit(solution)/shard_map/all_gather | solution.py:70
  76.4 31.8 %all_gather.18 = s32[32,1,12]{2,1,0:T(1,128)S(1)} all-gather(s32[1,1,12]{2,1,0:T(1,128)S(1)} %copy-done.7), channel_id=1, replica_groups=mesh['blk'=32,'ffn'=8] {'blk'}, dimensions={0}, use_global_device_ids=true | all-gather | bytes 1584 | tf_op jit(solution)/shard_map/all_gather | solution.py:79
  109.1 154.2 %while.32 = (s32[]{:T(128)}, f32[18,32768]{1,0:T(8,128)}, s32[384]{0:T(512)S(1)}, bf16[36,256,128]{2,1,0:T(8,128)(2,1)}, pred[384]{0:T(512)(128)(4,1)S(1)}, /*in...) while((s32[]{:T(128)}, f32[18,32768]{1,0:T(8,128)}, ...), condition=%wide.region_3.4_spmd.clone, body=%wide.region_2.3_spmd.clone.sunk | while | flops 745933568 | bytes 28317404 | solution.py:38
  117.4 10.2 %convolution_add_fusion.4 = f32[18,32768]{1,0:T(8,128)} fusion(f32[6,8,256,128]{3,2,1,0:T(8,128)} %bitcast.35, f32[18,32768]{1,0:T(8,128)} %get-tuple-element.534, pred[]{:T(512)S(6)} %compare.6, s32[48]{0:T(128)S(1)} %and_select_fusion.6), kind=kOutput, calls=%fused_computation.4.clone.1 | convolution fusion | flops 340919136 | bytes 11010241 | tf_op jit(solution)/shard_map/while/body/eval_jaxpr/nc,nk->ck/dot_general | solution.py:34
  130.8 5.2 fusion.45
  136.0 11.2 %convolution_add_fusion.4 = f32[18,32768]{1,0:T(8,128)} fusion(f32[6,8,256,128]{3,2,1,0:T(8,128)} %bitcast.35, f32[18,32768]{1,0:T(8,128)} %get-tuple-element.534, pred[]{:T(512)S(6)} %compare.6, s32[48]{0:T(128)S(1)} %and_select_fusion.6), kind=kOutput, calls=%fused_computation.4.clone.1 | convolution fusion | flops 340919136 | bytes 11010241 | tf_op jit(solution)/shard_map/while/body/eval_jaxpr/nc,nk->ck/dot_general | solution.py:34
  150.3 5.2 fusion.45
  155.6 11.2 %convolution_add_fusion.4 = f32[18,32768]{1,0:T(8,128)} fusion(f32[6,8,256,128]{3,2,1,0:T(8,128)} %bitcast.35, f32[18,32768]{1,0:T(8,128)} %get-tuple-element.534, pred[]{:T(512)S(6)} %compare.6, s32[48]{0:T(128)S(1)} %and_select_fusion.6), kind=kOutput, calls=%fused_computation.4.clone.1 | convolution fusion | flops 340919136 | bytes 11010241 | tf_op jit(solution)/shard_map/while/body/eval_jaxpr/nc,nk->ck/dot_general | solution.py:34
  175.1 11.0 %convolution_add_fusion.4 = f32[18,32768]{1,0:T(8,128)} fusion(f32[6,8,256,128]{3,2,1,0:T(8,128)} %bitcast.35, f32[18,32768]{1,0:T(8,128)} %get-tuple-element.534, pred[]{:T(512)S(6)} %compare.6, s32[48]{0:T(128)S(1)} %and_select_fusion.6), kind=kOutput, calls=%fused_computation.4.clone.1 | convolution fusion | flops 340919136 | bytes 11010241 | tf_op jit(solution)/shard_map/while/body/eval_jaxpr/nc,nk->ck/dot_general | solution.py:34
  194.4 11.0 %convolution_add_fusion.4 = f32[18,32768]{1,0:T(8,128)} fusion(f32[6,8,256,128]{3,2,1,0:T(8,128)} %bitcast.35, f32[18,32768]{1,0:T(8,128)} %get-tuple-element.534, pred[]{:T(512)S(6)} %compare.6, s32[48]{0:T(128)S(1)} %and_select_fusion.6), kind=kOutput, calls=%fused_computation.4.clone.1 | convolution fusion | flops 340919136 | bytes 11010241 | tf_op jit(solution)/shard_map/while/body/eval_jaxpr/nc,nk->ck/dot_general | solution.py:34
  213.7 11.0 %convolution_add_fusion.4 = f32[18,32768]{1,0:T(8,128)} fusion(f32[6,8,256,128]{3,2,1,0:T(8,128)} %bitcast.35, f32[18,32768]{1,0:T(8,128)} %get-tuple-element.534, pred[]{:T(512)S(6)} %compare.6, s32[48]{0:T(128)S(1)} %and_select_fusion.6), kind=kOutput, calls=%fused_computation.4.clone.1 | convolution fusion | flops 340919136 | bytes 11010241 | tf_op jit(solution)/shard_map/while/body/eval_jaxpr/nc,nk->ck/dot_general | solution.py:34
  233.0 11.0 %convolution_add_fusion.4 = f32[18,32768]{1,0:T(8,128)} fusion(f32[6,8,256,128]{3,2,1,0:T(8,128)} %bitcast.35, f32[18,32768]{1,0:T(8,128)} %get-tuple-element.534, pred[]{:T(512)S(6)} %compare.6, s32[48]{0:T(128)S(1)} %and_select_fusion.6), kind=kOutput, calls=%fused_computation.4.clone.1 | convolution fusion | flops 340919136 | bytes 11010241 | tf_op jit(solution)/shard_map/while/body/eval_jaxpr/nc,nk->ck/dot_general | solution.py:34
  252.2 11.0 %convolution_add_fusion.4 = f32[18,32768]{1,0:T(8,128)} fusion(f32[6,8,256,128]{3,2,1,0:T(8,128)} %bitcast.35, f32[18,32768]{1,0:T(8,128)} %get-tuple-element.534, pred[]{:T(512)S(6)} %compare.6, s32[48]{0:T(128)S(1)} %and_select_fusion.6), kind=kOutput, calls=%fused_computation.4.clone.1 | convolution fusion | flops 340919136 | bytes 11010241 | tf_op jit(solution)/shard_map/while/body/eval_jaxpr/nc,nk->ck/dot_general | solution.py:34
  267.1 168.5 %while.33 = (s32[]{:T(128)}, f32[36,32768]{1,0:T(8,128)}, s32[384]{0:T(512)S(1)}, bf16[18,256,128]{2,1,0:T(8,128)(2,1)}, pred[384]{0:T(512)(128)(4,1)S(1)}, /*in...) while((s32[]{:T(128)}, f32[36,32768]{1,0:T(8,128)}, ...), condition=%wide.region_5.6_spmd.clone, body=%wide.region_4.5_spmd.clone.sunk | while | flops 1086852736 | bytes 33035996 | solution.py:38
  274.9 12.0 %convolution_add_fusion.5 = f32[36,32768]{1,0:T(8,128)} fusion(f32[6,8,256,128]{3,2,1,0:T(8,128)} %bitcast.36, f32[36,32768]{1,0:T(8,128)} %get-tuple-element.564, pred[]{:T(512)S(6)} %compare.7, s32[48]{0:T(128)S(1)} %and_select_fusion.7), kind=kOutput, calls=%fused_computation.25.clone.1 | convolution fusion | flops 681838272 | bytes 15728833 | tf_op jit(solution)/shard_map/while/body/eval_jaxpr/nc,nk->ck/dot_general | solution.py:34
  294.6 13.5 %convolution_add_fusion.5 = f32[36,32768]{1,0:T(8,128)} fusion(f32[6,8,256,128]{3,2,1,0:T(8,128)} %bitcast.36, f32[36,32768]{1,0:T(8,128)} %get-tuple-element.564, pred[]{:T(512)S(6)} %compare.7, s32[48]{0:T(128)S(1)} %and_select_fusion.7), kind=kOutput, calls=%fused_computation.25.clone.1 | convolution fusion | flops 681838272 | bytes 15728833 | tf_op jit(solution)/shard_map/while/body/eval_jaxpr/nc,nk->ck/dot_general | solution.py:34
  315.9 13.5 %convolution_add_fusion.5 = f32[36,32768]{1,0:T(8,128)} fusion(f32[6,8,256,128]{3,2,1,0:T(8,128)} %bitcast.36, f32[36,32768]{1,0:T(8,128)} %get-tuple-element.564, pred[]{:T(512)S(6)} %compare.7, s32[48]{0:T(128)S(1)} %and_select_fusion.7), kind=kOutput, calls=%fused_computation.25.clone.1 | convolution fusion | flops 681838272 | bytes 15728833 | tf_op jit(solution)/shard_map/while/body/eval_jaxpr/nc,nk->ck/dot_general | solution.py:34
  337.1 13.5 %convolution_add_fusion.5 = f32[36,32768]{1,0:T(8,128)} fusion(f32[6,8,256,128]{3,2,1,0:T(8,128)} %bitcast.36, f32[36,32768]{1,0:T(8,128)} %get-tuple-element.564, pred[]{:T(512)S(6)} %compare.7, s32[48]{0:T(128)S(1)} %and_select_fusion.7), kind=kOutput, calls=%fused_computation.25.clone.1 | convolution fusion | flops 681838272 | bytes 15728833 | tf_op jit(solution)/shard_map/while/body/eval_jaxpr/nc,nk->ck/dot_general | solution.py:34
  358.4 13.5 %convolution_add_fusion.5 = f32[36,32768]{1,0:T(8,128)} fusion(f32[6,8,256,128]{3,2,1,0:T(8,128)} %bitcast.36, f32[36,32768]{1,0:T(8,128)} %get-tuple-element.564, pred[]{:T(512)S(6)} %compare.7, s32[48]{0:T(128)S(1)} %and_select_fusion.7), kind=kOutput, calls=%fused_computation.25.clone.1 | convolution fusion | flops 681838272 | bytes 15728833 | tf_op jit(solution)/shard_map/while/body/eval_jaxpr/nc,nk->ck/dot_general | solution.py:34
  379.6 13.5 %convolution_add_fusion.5 = f32[36,32768]{1,0:T(8,128)} fusion(f32[6,8,256,128]{3,2,1,0:T(8,128)} %bitcast.36, f32[36,32768]{1,0:T(8,128)} %get-tuple-element.564, pred[]{:T(512)S(6)} %compare.7, s32[48]{0:T(128)S(1)} %and_select_fusion.7), kind=kOutput, calls=%fused_computation.25.clone.1 | convolution fusion | flops 681838272 | bytes 15728833 | tf_op jit(solution)/shard_map/while/body/eval_jaxpr/nc,nk->ck/dot_general | solution.py:34
  400.9 13.5 %convolution_add_fusion.5 = f32[36,32768]{1,0:T(8,128)} fusion(f32[6,8,256,128]{3,2,1,0:T(8,128)} %bitcast.36, f32[36,32768]{1,0:T(8,128)} %get-tuple-element.564, pred[]{:T(512)S(6)} %compare.7, s32[48]{0:T(128)S(1)} %and_select_fusion.7), kind=kOutput, calls=%fused_computation.25.clone.1 | convolution fusion | flops 681838272 | bytes 15728833 | tf_op jit(solution)/shard_map/while/body/eval_jaxpr/nc,nk->ck/dot_general | solution.py:34
  422.1 13.5 %convolution_add_fusion.5 = f32[36,32768]{1,0:T(8,128)} fusion(f32[6,8,256,128]{3,2,1,0:T(8,128)} %bitcast.36, f32[36,32768]{1,0:T(8,128)} %get-tuple-element.564, pred[]{:T(512)S(6)} %compare.7, s32[48]{0:T(128)S(1)} %and_select_fusion.7), kind=kOutput, calls=%fused_computation.25.clone.1 | convolution fusion | flops 681838272 | bytes 15728833 | tf_op jit(solution)/shard_map/while/body/eval_jaxpr/nc,nk->ck/dot_general | solution.py:34
  447.7 76.4 %reduce-scatter.2.cloned.1.call-done = bf16[256,576]{0,1:T(8,128)(2,1)} async-done(((bf16[256,4608]{0,1:T(8,128)(2,1)}), bf16[256,576]{0,1:T(8,128)(2,1)}) %reduce-scatter.2.cloned.1.call-update) | async-done | bytes 294928 | tf_op jit(solution)/shard_map/reduce_scatter | solution.py:88
  (151 shorter events, 153.4 us)
Async XLA Ops:
  6.5 102.6 %all-gather.3.cloned.1.call-start = ((), (), s32[]{:S(2)}) async-start(), calls=%async_computation.1 | async-start | bytes 12976128 | tf_op jit(solution)/shard_map/all_gather | solution.py:69
  7.3 259.9 %all-gather.5.cloned.1.call-start = ((), (), s32[]{:S(2)}) async-start(), calls=%async_computation.2 | async-start | bytes 12976128 | tf_op jit(solution)/shard_map/all_gather | solution.py:78
  8.0 516.0 %reduce-scatter.2.cloned.1.call-start = ((), (), s32[]{:S(2)}) async-start(), calls=%async_computation.3 | async-start | bytes 2654208 | tf_op jit(solution)/shard_map/reduce_scatter | solution.py:88
  10.9 4.9 copy-start
  10.9 1.3 copy-start.2
  10.9 1.3 copy-start.3
  15.8 5.6 %copy-start.8 = (u32[256]{0:T(256)S(1)}, u32[256]{0:T(256)}, u32[]{:S(2)}) copy-start(u32[256]{0:T(256)} %constant.256) | copy-start | bytes 3076
  15.8 27.7 %copy-start.6 = (s32[1,1,12]{2,1,0:T(1,128)S(1)}, s32[1,1,12]{2,1,0:T(1,128)}, u32[]{:S(2)}) copy-start(s32[1,1,12]{2,1,0:T(1,128)} %param.19) | copy-start | bytes 148
  15.8 60.7 %copy-start.7 = (s32[1,1,12]{2,1,0:T(1,128)S(1)}, s32[1,1,12]{2,1,0:T(1,128)}, u32[]{:S(2)}) copy-start(s32[1,1,12]{2,1,0:T(1,128)} %param.23) | copy-start | bytes 148
  263.3 2.5 copy-start.4
  440.7 4.4 copy-start.1
  445.1 78.9 %copy-start.5 = (f32[576]{0:T(1024)S(1)}, f32[576]{0:T(1024)}, u32[]{:S(2)}) copy-start(f32[576]{0:T(1024)} %param.25) | copy-start | bytes 6916
Sparse Core Ops, SparseCore 0:
  9.2 83.2 all-gather.2
  94.3 80.0 all-gather.4
  445.2 78.7 reduce-scatter.1
where the time goes:
time: 534 us; the launch traced here: 533 us
  matrix products  276 us (52%)
  blocking collectives  83.2 us (16%)
  waiting for transfers between devices  77.8 us (15%)
  local copies, waits for them, and re-layouts  62.6 us (12%)
  other arithmetic  17.8 us (3%)
  between operations  14.6 us (3%)
    dot_general x16, matrix products, one_block(): jnp.einsum('nc,nk->ck', selector, flat_products, precision=lax.Precision....  194 us
    dot_general x16, matrix products, one_block(): jnp.einsum('nti,nij->ntj', inputs_now, tiles_now, preferred_element_type=...  81.8 us
    reduce_scatter x1, waiting for transfers between devices, on_device(): lax.psum_scatter(partial_value.astype(jnp.bfloat16), 'ffn', scatter_dimen...  76.4 us
    gather x16, local copies, waits for them, and re-layouts, one_block(): inputs_now = jnp.take(source_blocks, places_now // col_blocks, axis=0)  42.1 us
    all_gather x1, blocking collectives, on_device(): lax.all_gather(fc2_index, 'blk', axis=0, tiled=True)  31.8 us
    all_gather x1, blocking collectives, on_device(): lax.all_gather(fc1_index, 'blk', axis=0, tiled=True)  31.4 us
    unnamed x1, blocking collectives  19.9 us
  transfers between devices with their start and end apart: 3, of which 1 were waited for; matrix products, arithmetic and copies ran while one was open for 33% of the time, Pallas kernels for 0%

commit v1 on v0

v1 whole, which is shorter than its diff:
```python
import jax
import jax.numpy as jnp
from jax import lax
from jax.experimental import pallas as pl
from jax.experimental.pallas import tpu as pltpu
from jax.sharding import PartitionSpec as P

MESH = pl.DeviceIdType.MESH
TB = 128
SLOTS = 12
NP, NQ = 7, 5
ROWS, D, FFS = 256, 4608, 2304
RB, CB = 36, 18
SW = 640
TOT = 32 * SLOTS
F32, BF16 = jnp.float32, jnp.bfloat16


def kernel(
    tok_h, gain, beta, b1, b2, t1, t2, meta, out,
    G1, G2, M, Tv, Ts, tok, normed, hidden, S, R, RY,
    ls, ss, zA, zQ, yQ, yP, dS, mS, mY, mD, mZ, rS, rX, rY,
):
    b = lax.axis_index("blk")
    f = lax.axis_index("ffn")
    j, z, c = b // 16, (b // 2) % 8, b % 2
    yh, x = f // 4, f % 4
    tin, G = (t1, t2), (G1, G2)
    zdev = tuple({"blk": j * 16 + ((z + dz) % 8) * 2 + c} for dz in (1, 7))
    ydev = {"blk": (1 - j) * 16 + z * 2 + c}
    ddev = {"blk": j * 16 + z * 2 + (1 - c)}
    xdev = tuple({"ffn": yh * 4 + (x + dx) % 4} for dx in (1, 3))
    hdev = {"ffn": (1 - yh) * 4 + x}

    bar = pltpu.get_barrier_semaphore()
    for dev in (*zdev, ydev, ddev, *xdev, hdev):
        pl.semaphore_signal(bar, inc=1, device_id=dev, device_id_type=MESH)
    tok_cp = pltpu.make_async_copy(tok_h, tok, ls.at[2])
    tok_cp.start()
    pl.semaphore_wait(bar, 7)

    def send(src, dst, s_sem, r_sem, dev):
        pltpu.make_async_remote_copy(
            src_ref=src, dst_ref=dst, send_sem=s_sem, recv_sem=r_sem,
            device_id=dev, device_id_type=MESH,
        ).start()

    def got(ref, s_sem, r_sem, dev):
        pltpu.make_async_remote_copy(
            src_ref=ref, dst_ref=ref, send_sem=s_sem, recv_sem=r_sem,
            device_id=dev, device_id_type=MESH,
        ).wait_recv()

    def base(cc, jj, zz):
        return (cc * 16 + jj * 8 + zz) * SLOTS

    own = base(c, j, z)

    def start(q):
        g, t = G[q], tin[q]
        pltpu.make_async_copy(t, g.at[pl.ds(own, SLOTS)], ls.at[q]).start()
        for d in (0, 1):
            send(t, g.at[pl.ds(own, SLOTS)], ss.at[q], zA.at[q, d, 0], zdev[d])
        send(t.at[pl.ds(NP, NQ)], g.at[pl.ds(own + NP, NQ)], ss.at[q], yQ.at[q], ydev)
        send(t.at[pl.ds(0, NP)], g.at[pl.ds(own, NP)], ss.at[q], yP.at[q, 0], ydev)
        send(t, g.at[pl.ds(own, SLOTS)], ss.at[q], dS.at[q], ddev)

    def origin(d, s):
        return (z + (8 - s if d == 0 else s)) % 8

    def fwd(q, lo, n, r_sem, dev):
        ref = G[q].at[pl.ds(lo, n)]
        send(ref, ref, ss.at[q], r_sem, dev)

    def arrived(q, lo, n, r_sem, dev):
        got(G[q].at[pl.ds(lo, n)], ss.at[q], r_sem, dev)

    def relay(q, s):
        if s == 1:
            lo = base(c, 1 - j, z) + NP
            arrived(q, lo, NQ, yQ.at[q], ydev)
            for d in (0, 1):
                fwd(q, lo, NQ, zQ.at[q, d, 0], zdev[d])
            fwd(q, lo, NQ, dS.at[q], ddev)
        for d in (0, 1):
            lo = base(c, j, origin(d, s))
            if s < 4:
                arrived(q, lo, SLOTS, zA.at[q, d, s - 1], zdev[1 - d])
                if s < 3:
                    fwd(q, lo, SLOTS, zA.at[q, d, s], zdev[d])
                elif d == 0:
                    fwd(q, lo, NP, zA.at[q, d, s], zdev[d])
                else:
                    fwd(q, lo + NP, NQ, zA.at[q, d, s], zdev[d])
                fwd(q, lo, NP, yP.at[q, 2 * s - 1 + d], ydev)
                fwd(q, lo, SLOTS, dS.at[q], ddev)
            elif d == 0:
                arrived(q, lo, NP, zA.at[q, d, 3], zdev[1 - d])
                fwd(q, lo, NP, yP.at[q, 7], ydev)
                fwd(q, lo, NP, dS.at[q], ddev)
            else:
                arrived(q, lo + NP, NQ, zA.at[q, d, 3], zdev[1 - d])
                fwd(q, lo + NP, NQ, dS.at[q], ddev)
        for d in (0, 1):
            lo = base(c, 1 - j, origin(d, s)) + NP
            if s < 4:
                arrived(q, lo, NQ, zQ.at[q, d, s - 1], zdev[1 - d])
                if s < 3:
                    fwd(q, lo, NQ, zQ.at[q, d, s], zdev[d])
                elif d == 0:
                    fwd(q, lo, 2, zQ.at[q, d, s], zdev[d])
                else:
                    fwd(q, lo + 2, NQ - 2, zQ.at[q, d, s], zdev[d])
                fwd(q, lo, NQ, dS.at[q], ddev)
            elif d == 0:
                arrived(q, lo, 2, zQ.at[q, d, 3], zdev[1 - d])
                fwd(q, lo, 2, dS.at[q], ddev)
            else:
                arrived(q, lo + 2, NQ - 2, zQ.at[q, d, 3], zdev[1 - d])
                fwd(q, lo + 2, NQ - 2, dS.at[q], ddev)
        late = {1: ((0, 0),), 2: ((0, 1), (1, 1)), 3: ((0, 2), (1, 2)), 4: ((0, 3), (1, 3), (0, 4))}[s]
        for d, back in late:
            lo = base(c, 1 - j, origin(d, back) if back else z)
            arrived(q, lo, NP, yP.at[q, 2 * back - 1 + d if back else 0], ydev)
            fwd(q, lo, NP, dS.at[q], ddev)

    def m_at(zz, n=4):
        return M.at[pl.ds(zz * 4, n)]

    mine = M.at[pl.ds(z * 4 + c * 2 + j, 1)]
    pltpu.make_async_copy(meta, mine, ls.at[3]).start()
    send(meta, mine, mS, mY, ydev)
    start(0)
    pltpu.make_async_copy(meta, mine, ls.at[3]).wait()
    got(M.at[pl.ds(z * 4 + c * 2 + (1 - j), 1)], mS, mY, ydev)
    pair = M.at[pl.ds(z * 4 + c * 2, 2)]
    send(pair, pair, mS, mD, ddev)
    got(M.at[pl.ds(z * 4 + (1 - c) * 2, 2)], mS, mD, ddev)
    for d in (0, 1):
        send(m_at(z), m_at(z), mS, mZ.at[d, 0], zdev[d])

    def meta_relay(s):
        for d in (0, 1):
            if d == 1 and s == 4:
                continue
            at = m_at(origin(d, s))
            got(at, mS, mZ.at[d, s - 1], zdev[1 - d])
            if s + d < 4:
                send(at, at, mS, mZ.at[d, s], zdev[d])

    tok_cp.wait()

    def norm_rows(i, carry):
        rows = pl.ds(pl.multiple_of(i * 16, 16), 16)
        t = tok[rows, :].astype(F32)
        mu = jnp.mean(t, axis=1, keepdims=True)
        t = t - mu
        var = jnp.mean(t * t, axis=1, keepdims=True)
        normed[rows, :] = (t / jnp.sqrt(var + 1e-05) * gain[...] + beta[...]).astype(BF16)
        return carry

    lax.fori_loop(0, ROWS // 16, norm_rows, 0)
    zero_tile = jnp.zeros((TB, TB), BF16)
    G1[TOT] = zero_tile
    G2[TOT] = zero_tile

    relay(0, 1)
    meta_relay(1)
    relay(0, 2)
    meta_relay(2)
    relay(0, 3)
    start(1)
    meta_relay(3)
    meta_relay(4)

    m_id = lax.broadcasted_iota(jnp.int32, (32, TB), 0)
    first = ((m_id // 2 % 2) * 16 + (m_id % 2) * 8 + m_id // 4) * SLOTS
    lane = lax.broadcasted_iota(jnp.int32, (32, TB), 1)
    for q, (nr, nc) in enumerate(((RB, CB), (CB, RB))):
        seen = M[:, q, :]

        def row(r, carry):
            want = jnp.where(lane < nc, r * nc + lane, -2)
            best = jnp.full((32, TB), -1, jnp.int32)
            for s in range(SLOTS):
                best = jnp.where(seen[:, s : s + 1] == want, first + s, best)
            best = jnp.max(best, axis=0, keepdims=True)
            Tv[q, pl.ds(r, 1), :] = jnp.where(best < 0, TOT, best)
            return carry

        lax.fori_loop(0, nr, row, 0)
    tab_cp = pltpu.make_async_copy(Tv, Ts, ls.at[4])
    tab_cp.start()
    relay(0, 4)
    pltpu.make_async_copy(t1, G1.at[pl.ds(own, SLOTS)], ls.at[0]).wait()
    arrived(0, base(1 - c, 0, 0), TOT // 2, dS.at[0], ddev)
    tab_cp.wait()

    def block(g, q, r, col, wide):
        cols = []
        for w in range(wide):
            cols.append(jnp.concatenate([g[Ts[q, r, col + w]], g[Ts[q, r + 1, col + w]]], axis=0))
        return cols[0] if wide == 1 else jnp.concatenate(cols, axis=1)

    def product(src, g, q, chunks, col, wide):
        acc = None
        for k in range(chunks):
            part = jnp.dot(
                src[:, k * 256 : (k + 1) * 256], block(g, q, 2 * k, col, wide),
                preferred_element_type=F32,
            )
            acc = part if acc is None else acc + part
        return acc

    def fc1(p, carry):
        acc = product(normed, G1, 0, RB // 2, 2 * p, 2)
        cols = pl.ds(pl.multiple_of(p * 256, 256), 256)
        hidden[:, cols] = jnp.maximum(acc + b1[:, cols], 0.0).astype(BF16)
        return carry

    lax.fori_loop(0, 4, fc1, 0)
    relay(1, 1)
    lax.fori_loop(4, 9, fc1, 0)
    relay(1, 2)
    relay(1, 3)
    relay(1, 4)
    pltpu.make_async_copy(t2, G2.at[pl.ds(own, SLOTS)], ls.at[1]).wait()
    arrived(1, base(1 - c, 0, 0), TOT // 2, dS.at[1], ddev)

    def fc2(i, carry):
        d, step = i % 2, i // 2
        share = d * 4 + (x + 1 + step + (1 - d) * (2 - 2 * step)) % 4
        col = share // 2 * 9 + share % 2 * 4
        for w, wide in ((0, 2), (2, 2), (4, 1)):
            acc = product(hidden, G2, 1, CB // 2, col + w, wide)
            S[i, :, w * TB : (w + wide) * TB] = acc.astype(BF16)
        return carry

    H = ROWS // 2

    def ring(step):
        for h in (0, 1):
            for d in (0, 1):
                at = S.at[2 * step + d, pl.ds(h * H, H)]
                if step:
                    old = R.at[d, step - 1, pl.ds(h * H, H)]
                    got(old, rS, rX.at[d, step - 1, h], xdev[1 - d])
                    at[...] = (at[...].astype(F32) + old[...].astype(F32)).astype(BF16)
                send(at, R.at[d, step, pl.ds(h * H, H)], rS, rX.at[d, step, h], xdev[d])

    lax.fori_loop(0, 2, fc2, 0)
    ring(0)
    lax.fori_loop(2, 6, fc2, 0)
    ring(1)
    lax.fori_loop(6, 8, fc2, 0)
    ring(2)
    o = 1 - yh
    for h in (0, 1):
        rows = pl.ds(h * H, H)
        at, old = S.at[6 + o, rows], R.at[o, 2, rows]
        got(old, rS, rX.at[o, 2, h], xdev[0])
        at[...] = (at[...].astype(F32) + old[...].astype(F32)).astype(BF16)
        send(at, RY.at[rows], rS, rY.at[h], hdev)
    lo = pl.multiple_of((f // 2 * 9 + f % 2 * 4) * TB, TB)
    for h in (0, 1):
        rows = pl.ds(h * H, H)
        got(R.at[yh, 2, rows], rS, rX.at[yh, 2, h], xdev[0])
        got(RY.at[rows], rS, rY.at[h], hdev)
        sum_ = S[6 + yh, rows].astype(F32) + R[yh, 2, rows].astype(F32) + RY[rows].astype(F32)
        sum_ = sum_ + tok[rows, pl.ds(lo, SW)].astype(F32)

        @pl.when(f % 2 == 0)
        def _():
            out[rows, :] = (sum_[:, :576] + b2[...]).astype(BF16)

        @pl.when(f % 2 == 1)
        def _():
            out[rows, :] = (sum_[:, SW - 576 :] + b2[...]).astype(BF16)

    for q in (0, 1):
        all_sent = G[q].at[pl.ds(0, 372)]
        pltpu.make_async_remote_copy(
            src_ref=all_sent, dst_ref=all_sent, send_sem=ss.at[q], recv_sem=ss.at[q],
            device_id=ddev, device_id_type=MESH,
        ).wait_send()
    sent = S.at[pl.ds(0, 7)]
    pltpu.make_async_remote_copy(
        src_ref=sent, dst_ref=sent, send_sem=rS, recv_sem=rS, device_id=ddev, device_id_type=MESH,
    ).wait_send()
    for ref in (M.at[pl.ds(0, 31)],):
        pltpu.make_async_remote_copy(
            src_ref=ref, dst_ref=ref, send_sem=mS, recv_sem=mS, device_id=ddev, device_id_type=MESH,
        ).wait_send()


def on_device(tokens, gain, beta, t1, i1, n1, b1, t2, i2, n2, b2):
    def listed(index, count):
        live = jnp.arange(SLOTS, dtype=jnp.int32) < count.reshape(1)
        return jnp.pad(jnp.where(live, index.reshape(SLOTS), -1), (0, TB - SLOTS), constant_values=-1)

    meta = jnp.pad(jnp.stack([listed(i1, n1), listed(i2, n2)]), ((0, 6), (0, 0)))[None]
    vm = pl.BlockSpec(memory_space=pltpu.VMEM)
    hb = pl.BlockSpec(memory_space=pl.ANY)
    dma, V = pltpu.SemaphoreType.DMA, pltpu.VMEM
    return pl.pallas_call(
        kernel,
        out_shape=jax.ShapeDtypeStruct((ROWS, 576), BF16),
        in_specs=[hb, vm, vm, vm, vm, hb, hb, hb],
        out_specs=vm,
        scratch_shapes=[
            V((TOT + 1, TB, TB), BF16),
            V((TOT + 1, TB, TB), BF16),
            V((32, 8, TB), jnp.int32),
            V((2, 40, TB), jnp.int32),
            pltpu.SMEM((2, 40, TB), jnp.int32),
            V((ROWS, D), BF16),
            V((ROWS, D), BF16),
            V((ROWS, FFS), BF16),
            V((8, ROWS, SW), BF16),
            V((2, 3, ROWS, SW), BF16),
            V((ROWS, SW), BF16),
            dma((5,)),
            dma((2,)),
            dma((2, 2, 4)),
            dma((2, 2, 4)),
            dma((2,)),
            dma((2, 8)),
            dma((2,)),
            dma,
            dma,
            dma,
            dma((2, 4)),
            dma,
            dma((2, 3, 2)),
            dma((2,)),
        ],
        compiler_params=pltpu.CompilerParams(
            collective_id=0, has_side_effects=True, vmem_limit_bytes=60 * 1024 * 1024
        ),
    )(
        tokens, gain.reshape(1, D), beta.reshape(1, D), b1.reshape(1, FFS), b2.reshape(1, 576),
        t1.reshape(SLOTS, TB, TB), t2.reshape(SLOTS, TB, TB), meta,
    )


def solution(mesh):
    tile, pair = P("blk", "ffn", None, None, None), P("blk", "ffn")
    placed = (
        P("blk", None), P(), P(), tile, P("blk", "ffn", None), pair, P("ffn"),
        tile, P("blk", "ffn", None), pair, P("ffn"),
    )
    return jax.shard_map(
        on_device, mesh=mesh, in_specs=placed, out_specs=P("blk", "ffn"), check_vma=False
    )
```

time: 534 us -> 190 us (0.36)
  matrix products: 276 us -> 0 us
  Pallas kernels: 0 us -> 178 us
  blocking collectives: 83.2 us -> 0 us
  waiting for transfers between devices: 77.8 us -> 0 us
  local copies, waits for them, and re-layouts: 62.6 us -> 7.7 us
  other arithmetic: 17.8 us -> 1.33 us
  between operations: 14.6 us -> 1.31 us
    dot_general x32 -> x0, matrix products: 276 us -> none  [the longest x16 194 us: one_block(): jnp.einsum('nc,nk->ck', selector, flat_products, precision=lax.Precision....]
    pallas_call x0 -> x1, Pallas kernels: none -> 178 us  [on_device(): pl.pallas_call(kernel, out_shape=jax.ShapeDtypeStruct((ROWS, 576), BF16),...]
    reduce_scatter x1 -> x0, waiting for transfers between devices: 76.4 us -> none  [on_device(): lax.psum_scatter(partial_value.astype(jnp.bfloat16), 'ffn', scatter_dimen...]
    all_gather x2 -> x0, blocking collectives: 63.3 us -> none  [the longest x1 31.8 us: on_device(): lax.all_gather(fc2_index, 'blk', axis=0, tiled=True)]
    gather x16 -> x0, local copies, waits for them, and re-layouts: 42.1 us -> none  [one_block(): inputs_now = jnp.take(source_blocks, places_now // col_blocks, axis=0)]
    unnamed x1 -> x0, blocking collectives: 19.9 us -> none
    convert_element_type x5 -> x0, other arithmetic: 12.1 us -> none  [the longest x1 3.49 us: on_device(): ((rows_f - center) / jnp.sqrt(spread + 1e-05) * ln_gain + ln_bias).astype...]
    unnamed x26 -> x0, local copies, waits for them, and re-layouts: 7.88 us -> none
  transfers between devices with their start and end apart: 3 -> 0, of which waited for: 1 -> 0; matrix products, arithmetic and copies ran while one was open for 33% -> 0% of each run, Pallas kernels for 0% -> 0%
where the time goes in v1:
time: 190 us; the launch traced here: 188 us
  Pallas kernels  178 us (94%)
  local copies, waits for them, and re-layouts  7.7 us (4%)
    pallas_call x1, Pallas kernels, on_device(): pl.pallas_call(kernel, out_shape=jax.ShapeDtypeStruct((ROWS, 576), BF16),...  178 us

profile of v1, /device:TPU:2, one launch (start us, length us, event | category | flops | bytes accessed | tf_op | source)
XLA Modules:
  0.0 188.0 jit_solution(9874777064310362184)
XLA Ops:
  1.3 0.7 compare_select_fusion
  2.0 0.7 compare_select_fusion.1
  2.6 1.3 reshape.31.b2
  3.9 0.6 pad_bitcast_fusion.meta
  4.5 1.3 reshape.30.b1
  5.8 1.3 reshape.28.gain
  7.1 1.3 reshape.29.beta
  8.5 177.7 %shard_map.109 = bf16[256,576]{1,0:T(8,128)(2,1)} custom-call(bf16[256,4608]{1,0:T(8,128)(2,1)} %tok_h.1, f32[1,4608]{1,0:T(1,128)} %reshape.28.gain, f32[1,4608]{1,0:T(1,128)} %reshape.29.beta, f32[1,2304]{1,0:T(1,128)} %reshape.30.b1, f32[1,576]{1,0:T(1,128)} %reshape.31.b2, bf16[12,128,128]{2,1,0:T(8,128)(2,1)} %bitcast.16, ...), custom_call_target="tpu_custom_call" | custom-call | tf_op jit(solution)/shard_map/pallas_call | solution.py:305
  186.2 1.8 copy.12
  (2 shorter events, 0.0 us)

commit v2 on v1

v2 whole, which is shorter than its diff:
```python
import jax
import jax.numpy as jnp
from jax import lax
from jax.experimental import pallas as pl
from jax.experimental.pallas import tpu as pltpu
from jax.sharding import PartitionSpec as P

MESH = pl.DeviceIdType.MESH
TB = 128
SLOTS = 12
NP, NQ = 7, 5
FAR = (2, 3)
ROWS, D, FFS = 256, 4608, 2304
RB, CB = 36, 18
SW = 640
SR = 1152
TOT = 32 * SLOTS
F32, BF16 = jnp.float32, jnp.bfloat16


def kernel(
    tok_h, gain, beta, b1, b2, t1, t2, i1, n1, i2, n2, out,
    G1, G2, M, Tv, Ts, tok, normed, hidden, S, R, RY, W,
    ls, ss, zA, zQ, yQ, yP, dS, mS, mY, mD, mZ, rS, rX, rY,
):
    b = lax.axis_index("blk")
    f = lax.axis_index("ffn")
    j, z, c = b // 16, (b // 2) % 8, b % 2
    yh, x = f // 4, f % 4
    tin, G = (t1, t2), (G1, G2)
    zdev = tuple({"blk": j * 16 + ((z + dz) % 8) * 2 + c} for dz in (1, 7))
    ydev = {"blk": (1 - j) * 16 + z * 2 + c}
    ddev = {"blk": j * 16 + z * 2 + (1 - c)}
    xdev = tuple({"ffn": yh * 4 + (x + dx) % 4} for dx in (1, 3))
    hdev = {"ffn": (1 - yh) * 4 + x}

    bar = pltpu.get_barrier_semaphore()
    for dev in (*zdev, ydev, ddev, *xdev, hdev):
        pl.semaphore_signal(bar, inc=1, device_id=dev, device_id_type=MESH)
    tok_cp = pltpu.make_async_copy(tok_h, tok, ls.at[2])
    tok_cp.start()
    sub = lax.broadcasted_iota(jnp.int32, (8, TB), 0)
    lane8 = lax.broadcasted_iota(jnp.int32, (8, TB), 1)
    seen = jnp.full((8, TB), -1, jnp.int32)
    for q, (idx, num) in enumerate(((i1, n1), (i2, n2))):
        for s in range(SLOTS):
            here = (sub == q) & (lane8 == s) & (s < num[0, 0])
            seen = jnp.where(here, idx[0, 0, s], seen)
    M[z * 4 + c * 2 + j] = seen
    pl.semaphore_wait(bar, 7)

    def send(src, dst, s_sem, r_sem, dev):
        pltpu.make_async_remote_copy(
            src_ref=src, dst_ref=dst, send_sem=s_sem, recv_sem=r_sem,
            device_id=dev, device_id_type=MESH,
        ).start()

    def got(ref, s_sem, r_sem, dev):
        pltpu.make_async_remote_copy(
            src_ref=ref, dst_ref=ref, send_sem=s_sem, recv_sem=r_sem,
            device_id=dev, device_id_type=MESH,
        ).wait_recv()

    def base(cc, jj, zz):
        return (cc * 16 + jj * 8 + zz) * SLOTS

    own = base(c, j, z)

    def start_y(q):
        g, t = G[q], tin[q]
        send(t.at[pl.ds(NP, NQ)], g.at[pl.ds(own + NP, NQ)], ss.at[q], yQ.at[q], ydev)
        send(t.at[pl.ds(0, NP)], g.at[pl.ds(own, NP)], ss.at[q], yP.at[q, 0], ydev)

    def start_z(q):
        g, t = G[q], tin[q]
        for k, (lo, n) in enumerate(((0, NP), (NP, NQ))):
            for d in (0, 1):
                send(t.at[pl.ds(lo, n)], g.at[pl.ds(own + lo, n)], ss.at[q], zA.at[q, d, 0, k], zdev[d])
        send(t, g.at[pl.ds(own, SLOTS)], ss.at[q], dS.at[q], ddev)
        pltpu.make_async_copy(t, g.at[pl.ds(own, SLOTS)], ls.at[q]).start()

    def origin(d, s):
        return (z + (8 - s if d == 0 else s)) % 8

    def fwd(q, lo, n, r_sem, dev):
        ref = G[q].at[pl.ds(lo, n)]
        send(ref, ref, ss.at[q], r_sem, dev)

    def arrived(q, lo, n, r_sem, dev):
        got(G[q].at[pl.ds(lo, n)], ss.at[q], r_sem, dev)

    def a_part(q, d, s, k):
        lo, n = base(c, j, origin(d, s)) + (NP if k else 0), (NQ if k else NP)
        arrived(q, lo, n, zA.at[q, d, s - 1, k], zdev[1 - d])
        if s < 3 or (s == 3 and d == k):
            fwd(q, lo, n, zA.at[q, d, s, k], zdev[d])
        if not k:
            fwd(q, lo, n, yP.at[q, 2 * s - 1 + d], ydev)
        fwd(q, lo, n, dS.at[q], ddev)

    def a_step(q, s):
        for k in (0, 1):
            for d in (0, 1):
                if s < 4 or d == k:
                    a_part(q, d, s, k)

    def q_at(d, s, half):
        lo = base(c, 1 - j, origin(d, s)) + NP
        if half is None:
            return lo, NQ
        return (lo, FAR[0]) if d != half else (lo + FAR[0], FAR[1])

    def q_own(q):
        lo = base(c, 1 - j, z) + NP
        for d in (0, 1):
            fwd(q, lo, NQ, zQ.at[q, d, 0, 0], zdev[d])

    def q_step(q, s):
        for half in (1, 0) if s == 3 else (1,) if s == 4 else (None,):
            for d in (0, 1):
                lo, n = q_at(d, s, half)
                arrived(q, lo, n, zQ.at[q, d, s - 1, 1 if half == 0 else 0], zdev[1 - d])
                if s == 1:
                    fwd(q, lo, n, zQ.at[q, d, 1, 0], zdev[d])
                if s == 2:
                    for h in (1, 0):
                        lo2, n2 = q_at(d, s, h)
                        fwd(q, lo2, n2, zQ.at[q, d, 2, 1 - h], zdev[d])
                if s == 3 and half == 1:
                    fwd(q, lo, n, zQ.at[q, d, 3, 0], zdev[d])
                fwd(q, lo, n, dS.at[q], ddev)

    def y_q(q):
        lo = base(c, 1 - j, z) + NP
        arrived(q, lo, NQ, yQ.at[q], ydev)
        fwd(q, lo, NQ, dS.at[q], ddev)

    def y_p(q, d, back):
        lo = base(c, 1 - j, origin(d, back) if back else z)
        arrived(q, lo, NP, yP.at[q, 2 * back - 1 + d if back else 0], ydev)
        fwd(q, lo, NP, dS.at[q], ddev)

    def m_at(zz, n=4):
        return M.at[pl.ds(zz * 4, n)]

    at = pl.ds(z * 4 + c * 2 + j, 1)
    send(M.at[at], M.at[at], mS, mY, ydev)
    start_y(0)
    start_z(0)
    got(M.at[pl.ds(z * 4 + c * 2 + (1 - j), 1)], mS, mY, ydev)
    both = M.at[pl.ds(z * 4 + c * 2, 2)]
    send(both, both, mS, mD, ddev)
    got(M.at[pl.ds(z * 4 + (1 - c) * 2, 2)], mS, mD, ddev)
    for d in (0, 1):
        send(m_at(z), m_at(z), mS, mZ.at[d, 0], zdev[d])

    def meta_relay(s):
        for d in (0, 1):
            if d == 1 and s == 4:
                continue
            at = m_at(origin(d, s))
            got(at, mS, mZ.at[d, s - 1], zdev[1 - d])
            if s + d < 4:
                send(at, at, mS, mZ.at[d, s], zdev[d])

    tok_cp.wait()

    def norm_rows(i, carry):
        rows = pl.ds(pl.multiple_of(i * 16, 16), 16)
        t = tok[rows, :].astype(F32)
        t = t - jnp.mean(t, axis=1, keepdims=True)
        var = jnp.mean(t * t, axis=1, keepdims=True)
        t = t * (1.0 / jnp.sqrt(var + 1e-05))
        normed[rows, :] = (t * gain[...][None] + beta[...][None]).astype(BF16)
        return carry

    lax.fori_loop(0, ROWS // 16, norm_rows, 0)
    zero_tile = jnp.zeros((TB, TB), BF16)
    G1[TOT] = zero_tile
    G2[TOT] = zero_tile

    y_q(0)
    a_step(0, 1)
    q_own(0)
    meta_relay(1)
    y_p(0, 0, 0)
    a_step(0, 2)
    meta_relay(2)
    q_step(0, 1)
    y_p(0, 0, 1)
    y_p(0, 1, 1)
    a_step(0, 3)
    start_y(1)
    meta_relay(3)
    q_step(0, 2)
    y_p(0, 0, 2)
    y_p(0, 1, 2)
    a_step(0, 4)
    start_z(1)
    meta_relay(4)

    m_id = lax.broadcasted_iota(jnp.int32, (32, TB), 0)
    first = ((m_id // 2 % 2) * 16 + (m_id % 2) * 8 + m_id // 4) * SLOTS
    lane = lax.broadcasted_iota(jnp.int32, (32, TB), 1)
    for q, (nr, nc) in enumerate(((RB, CB), (CB, RB))):
        listed = M[:, q, :]
        for s in range(SLOTS):
            W[s] = jnp.broadcast_to(listed[:, s : s + 1], (32, TB))

        def row(r, carry):
            want = jnp.where(lane < nc, r * nc + lane, -2)
            best = jnp.full((32, TB), -1, jnp.int32)
            for s in range(SLOTS):
                best = jnp.where(W[s] == want, first + s, best)
            best = jnp.max(best, axis=0, keepdims=True)
            Tv[q, pl.ds(r, 1), :] = jnp.where(best < 0, TOT, best)
            return carry

        lax.fori_loop(0, nr, row, 0)
    tab_cp = pltpu.make_async_copy(Tv, Ts, ls.at[4])
    tab_cp.start()
    q_step(0, 3)
    y_p(0, 0, 3)
    y_p(0, 1, 3)
    q_step(0, 4)
    y_p(0, 0, 4)
    y_q(1)
    pltpu.make_async_copy(t1, G1.at[pl.ds(own, SLOTS)], ls.at[0]).wait()
    arrived(0, base(1 - c, 0, 0), TOT // 2, dS.at[0], ddev)
    tab_cp.wait()

    def block(g, q, r, col, wide):
        cols = []
        for w in range(wide):
            cols.append(jnp.concatenate([g[Ts[q, r, col + w]], g[Ts[q, r + 1, col + w]]], axis=0))
        return cols[0] if wide == 1 else jnp.concatenate(cols, axis=1)

    def product(src, g, q, chunks, col, wide):
        acc = None
        for k in range(chunks):
            part = jnp.dot(
                src[:, k * 256 : (k + 1) * 256], block(g, q, 2 * k, col, wide),
                preferred_element_type=F32,
            )
            acc = part if acc is None else acc + part
        return acc

    def fc1(p, carry):
        acc = product(normed, G1, 0, RB // 2, 2 * p, 2)
        cols = pl.ds(pl.multiple_of(p * 256, 256), 256)
        hidden[:, cols] = jnp.maximum(acc + b1[cols][None], 0.0).astype(BF16)
        return carry

    a_step(1, 1)
    q_own(1)
    y_p(1, 0, 0)
    lax.fori_loop(0, 3, fc1, 0)
    a_step(1, 2)
    lax.fori_loop(3, 5, fc1, 0)
    q_step(1, 1)
    y_p(1, 0, 1)
    y_p(1, 1, 1)
    lax.fori_loop(5, 7, fc1, 0)
    a_step(1, 3)
    lax.fori_loop(7, 9, fc1, 0)
    q_step(1, 2)
    y_p(1, 0, 2)
    y_p(1, 1, 2)
    a_step(1, 4)
    q_step(1, 3)
    y_p(1, 0, 3)
    y_p(1, 1, 3)
    q_step(1, 4)
    y_p(1, 0, 4)
    pltpu.make_async_copy(t2, G2.at[pl.ds(own, SLOTS)], ls.at[1]).wait()
    arrived(1, base(1 - c, 0, 0), TOT // 2, dS.at[1], ddev)

    def fc2(i, carry):
        d, step = i % 2, i // 2
        share = d * 4 + (x + 1 + step + (1 - d) * (2 - 2 * step)) % 4
        pair, odd = share // 2 * 9, share % 2
        for w in (0, 2):
            acc = product(hidden, G2, 1, CB // 2, pair + odd * 5 + w, 2).astype(BF16)
            S[i, w * ROWS : (w + 1) * ROWS] = acc[:, :TB]
            S[i, (w + 1) * ROWS : (w + 2) * ROWS] = acc[:, TB:]
        acc = product(hidden, G2, 1, CB // 2, pair + 4, 1)
        top, low = acc[: ROWS // 2], acc[ROWS // 2 :]
        left = lax.broadcasted_iota(jnp.int32, (ROWS // 2, TB), 1) < TB // 2
        turned = pltpu.roll(jnp.where(odd == 1, top, low), TB // 2, 1)
        half = jnp.where(left == (odd == 1), turned, jnp.where(odd == 1, low, top))
        S[i, 4 * ROWS :] = half.astype(BF16)
        return carry

    H = SR // 2

    def ring(step):
        for h in (0, 1):
            for d in (0, 1):
                at = S.at[2 * step + d, pl.ds(h * H, H)]
                if step:
                    old = R.at[d, step - 1, pl.ds(h * H, H)]
                    got(old, rS, rX.at[d, step - 1, h], xdev[1 - d])
                    at[...] = (at[...].astype(F32) + old[...].astype(F32)).astype(BF16)
                send(at, R.at[d, step, pl.ds(h * H, H)], rS, rX.at[d, step, h], xdev[d])

    lax.fori_loop(0, 2, fc2, 0)
    ring(0)
    lax.fori_loop(2, 6, fc2, 0)
    ring(1)
    lax.fori_loop(6, 8, fc2, 0)
    ring(2)
    o = 1 - yh
    for h in (0, 1):
        rows = pl.ds(h * H, H)
        at, old = S.at[6 + o, rows], R.at[o, 2, rows]
        got(old, rS, rX.at[o, 2, h], xdev[0])
        at[...] = (at[...].astype(F32) + old[...].astype(F32)).astype(BF16)
        send(at, RY.at[rows], rS, rY.at[h], hdev)
    lo = pl.multiple_of((f // 2 * 9 + f % 2 * 4) * TB, TB)
    for h in (0, 1):
        rows = pl.ds(h * H, H)
        got(R.at[yh, 2, rows], rS, rX.at[yh, 2, h], xdev[0])
        got(RY.at[rows], rS, rY.at[h], hdev)
    total = S[6 + yh].astype(F32) + R[yh, 2].astype(F32) + RY[...].astype(F32)
    main = [total[w * ROWS : (w + 1) * ROWS] for w in range(4)]
    half = total[4 * ROWS :]
    turned = pltpu.roll(half, TB // 2, 1)

    @pl.when(f % 2 == 0)
    def _():
        full = jnp.concatenate(main + [jnp.concatenate([half, turned], axis=0)], axis=1)
        full = full + tok[:, pl.ds(lo, SW)].astype(F32)
        out[...] = (full[:, :576] + b2[...][None]).astype(BF16)

    @pl.when(f % 2 == 1)
    def _():
        full = jnp.concatenate([jnp.concatenate([turned, half], axis=0)] + main, axis=1)
        full = full + tok[:, pl.ds(lo, SW)].astype(F32)
        out[...] = (full[:, SW - 576 :] + b2[...][None]).astype(BF16)

    for q in (0, 1):
        all_sent = G[q].at[pl.ds(0, 372)]
        pltpu.make_async_remote_copy(
            src_ref=all_sent, dst_ref=all_sent, send_sem=ss.at[q], recv_sem=ss.at[q],
            device_id=ddev, device_id_type=MESH,
        ).wait_send()
    sent = S.at[pl.ds(0, 7)]
    pltpu.make_async_remote_copy(
        src_ref=sent, dst_ref=sent, send_sem=rS, recv_sem=rS, device_id=ddev, device_id_type=MESH,
    ).wait_send()
    ref = M.at[pl.ds(0, 31)]
    pltpu.make_async_remote_copy(
        src_ref=ref, dst_ref=ref, send_sem=mS, recv_sem=mS, device_id=ddev, device_id_type=MESH,
    ).wait_send()


def on_device(tokens, gain, beta, t1, i1, n1, b1, t2, i2, n2, b2):
    vm = pl.BlockSpec(memory_space=pltpu.VMEM)
    hb = pl.BlockSpec(memory_space=pl.ANY)
    sm = pl.BlockSpec(memory_space=pltpu.SMEM)
    dma, V = pltpu.SemaphoreType.DMA, pltpu.VMEM
    return pl.pallas_call(
        kernel,
        out_shape=jax.ShapeDtypeStruct((ROWS, 576), BF16),
        in_specs=[hb, vm, vm, vm, vm, hb, hb, sm, sm, sm, sm],
        out_specs=vm,
        scratch_shapes=[
            V((TOT + 1, TB, TB), BF16),
            V((TOT + 1, TB, TB), BF16),
            V((32, 8, TB), jnp.int32),
            V((2, 40, TB), jnp.int32),
            pltpu.SMEM((2, 40, TB), jnp.int32),
            V((ROWS, D), BF16),
            V((ROWS, D), BF16),
            V((ROWS, FFS), BF16),
            V((8, SR, TB), BF16),
            V((2, 3, SR, TB), BF16),
            V((SR, TB), BF16),
            V((SLOTS, 32, TB), jnp.int32),
            dma((5,)),
            dma((2,)),
            dma((2, 2, 4, 2)),
            dma((2, 2, 4, 2)),
            dma((2,)),
            dma((2, 8)),
            dma((2,)),
            dma,
            dma,
            dma,
            dma((2, 4)),
            dma,
            dma((2, 3, 2)),
            dma((2,)),
        ],
        compiler_params=pltpu.CompilerParams(
            collective_id=0, has_side_effects=True, vmem_limit_bytes=60 * 1024 * 1024
        ),
    )(
        tokens, gain, beta, b1, b2, t1.reshape(SLOTS, TB, TB), t2.reshape(SLOTS, TB, TB), i1, n1, i2, n2,
    )


def solution(mesh):
    tile, pair = P("blk", "ffn", None, None, None), P("blk", "ffn")
    placed = (
        P("blk", None), P(), P(), tile, P("blk", "ffn", None), pair, P("ffn"),
        tile, P("blk", "ffn", None), pair, P("ffn"),
    )
    return jax.shard_map(
        on_device, mesh=mesh, in_specs=placed, out_specs=P("blk", "ffn"), check_vma=False
    )
```

time: 190 us -> 140 us (0.74)
  Pallas kernels: 178 us -> 135 us
  local copies, waits for them, and re-layouts: 7.7 us -> 1.84 us
    pallas_call x1, Pallas kernels: 178 us -> 135 us  [on_device(): pl.pallas_call(kernel, out_shape=jax.ShapeDtypeStruct((ROWS, 576), BF16),...]
    reshape x4 -> x0, local copies, waits for them, and re-layouts: 5.27 us -> none  [the longest x1 1.35 us: on_device(): gain.reshape(1, D)]
where the time goes in v2:
time: 140 us; the launch traced here: 138 us
  Pallas kernels  135 us (96%)
  local copies, waits for them, and re-layouts  1.84 us (1%)
    pallas_call x1, Pallas kernels, on_device(): pl.pallas_call(kernel, out_shape=jax.ShapeDtypeStruct((ROWS, 576), BF16),...  135 us

profile of v2, /device:TPU:2, one launch (start us, length us, event | category | flops | bytes accessed | tf_op | source)
XLA Modules:
  0.0 138.3 jit_solution(10960857366108585942)
XLA Ops:
  1.3 135.1 %shard_map.109 = bf16[256,576]{1,0:T(8,128)(2,1)} custom-call(bf16[256,4608]{1,0:T(8,128)(2,1)} %tok_h.1, f32[4608]{0:T(1024)} %gain.1, f32[4608]{0:T(1024)} %beta.1, f32[2304]{0:T(1024)} %b1.1, f32[576]{0:T(1024)} %b2.1, bf16[12,128,128]{2,1,0:T(8,128)(2,1)} %bitcast.2, bf16[12,128,128]{2,1,0:T(8,128)(2,1)} %bitcast.3, s32[1,1,12]{2,1,0:T(1,128)} %i1.1, ...), custom_call_target="tpu_custom_call" | custom-call | tf_op jit(solution)/shard_map/pallas_call | solution.py:362
  136.4 1.8 %copy.12 = bf16[256,576]{0,1:T(8,128)(2,1)} copy(bf16[256,576]{1,0:T(8,128)(2,1)} %shard_map.109) | data formatting | bytes 589824 | tf_op jit(solution)/shard_map/pallas_call | solution.py:362

commit v3 on v2

--- a/solution.py
+++ b/solution.py
@@ -1,3 +1,5 @@
+import functools
+
 import jax
 import jax.numpy as jnp
 from jax import lax
@@ -14,14 +16,15 @@
 RB, CB = 36, 18
 SW = 640
 SR = 1152
+SB = 512
 TOT = 32 * SLOTS
 F32, BF16 = jnp.float32, jnp.bfloat16
 
 
 def kernel(
-    tok_h, gain, beta, b1, b2, t1, t2, i1, n1, i2, n2, out,
-    G1, G2, M, Tv, Ts, tok, normed, hidden, S, R, RY, W,
-    ls, ss, zA, zQ, yQ, yP, dS, mS, mY, mD, mZ, rS, rX, rY,
+    tok_h, gain, beta, b1, b2, t1, t2, i1, c1, i2, c2, out,
+    G1, G2, M, Tv, Ts, tok, normed, hidden, S, R, RY, YB, Q, W, n1, n2,
+    ls, ss, zA, zQ, yQ, yP, dS, mS, mY, mD, mZ, rS, rX, rY, rB, rQ,
 ):
     b = lax.axis_index("blk")
     f = lax.axis_index("ffn")
@@ -39,9 +42,14 @@
         pl.semaphore_signal(bar, inc=1, device_id=dev, device_id_type=MESH)
     tok_cp = pltpu.make_async_copy(tok_h, tok, ls.at[2])
     tok_cp.start()
+    counts = [pltpu.make_async_copy(h, num, ls.at[5 + k]) for k, (h, num) in enumerate(((c1, n1), (c2, n2)))]
+    for cp in counts:
+        cp.start()
     sub = lax.broadcasted_iota(jnp.int32, (8, TB), 0)
     lane8 = lax.broadcasted_iota(jnp.int32, (8, TB), 1)
     seen = jnp.full((8, TB), -1, jnp.int32)
+    for cp in counts:
+        cp.wait()
     for q, (idx, num) in enumerate(((i1, n1), (i2, n2))):
         for s in range(SLOTS):
             here = (sub == q) & (lane8 == s) & (s < num[0, 0])
@@ -91,9 +99,20 @@
 
     def a_part(q, d, s, k):
         lo, n = base(c, j, origin(d, s)) + (NP if k else 0), (NQ if k else NP)
+        far = ((lo, 4, 0), (lo + 4, n - 4, 1)) if d == k == 0 else ((lo, n, k),)
+        if s == 4:
+            for at, m, u in far:
+                arrived(q, at, m, zA.at[q, d, 3, u], zdev[1 - d])
+                if not k:
+                    fwd(q, at, m, yP.at[q, 7 + u], ydev)
+                fwd(q, at, m, dS.at[q], ddev)
+            return
         arrived(q, lo, n, zA.at[q, d, s - 1, k], zdev[1 - d])
-        if s < 3 or (s == 3 and d == k):
+        if s < 3:
             fwd(q, lo, n, zA.at[q, d, s, k], zdev[d])
+        elif d == k:
+            for at, m, u in far:
+                fwd(q, at, m, zA.at[q, d, 3, u], zdev[d])
         if not k:
             fwd(q, lo, n, yP.at[q, 2 * s - 1 + d], ydev)
         fwd(q, lo, n, dS.at[q], ddev)
@@ -137,8 +156,9 @@
 
     def y_p(q, d, back):
         lo = base(c, 1 - j, origin(d, back) if back else z)
-        arrived(q, lo, NP, yP.at[q, 2 * back - 1 + d if back else 0], ydev)
-        fwd(q, lo, NP, dS.at[q], ddev)
+        for at, m, u in ((lo, 4, 7), (lo + 4, NP - 4, 8)) if back == 4 else ((lo, NP, 2 * back - 1 + d if back else 0),):
+            arrived(q, at, m, yP.at[q, u], ydev)
+            fwd(q, at, m, dS.at[q], ddev)
 
     def m_at(zz, n=4):
         return M.at[pl.ds(zz * 4, n)]
@@ -275,14 +295,21 @@
     pltpu.make_async_copy(t2, G2.at[pl.ds(own, SLOTS)], ls.at[1]).wait()
     arrived(1, base(1 - c, 0, 0), TOT // 2, dS.at[1], ddev)
 
-    def fc2(i, carry):
-        d, step = i % 2, i // 2
-        share = d * 4 + (x + 1 + step + (1 - d) * (2 - 2 * step)) % 4
+    def fc2(early, i, carry):
+        order = ((3, 0), (1, 1), (1, 0), (3, 1), (2, 0), (2, 1), (0, 0), (0, 1))
+        off, d = jnp.int32(0), i % 2
+        for at, (o, k) in enumerate(order):
+            off = jnp.where(i == at, o, off)
+            d = jnp.where(i == at, k, d)
+        i = 2 * off + d
+        share = d * 4 + (x + off) % 4
         pair, odd = share // 2 * 9, share % 2
-        for w in (0, 2):
-            acc = product(hidden, G2, 1, CB // 2, pair + odd * 5 + w, 2).astype(BF16)
-            S[i, w * ROWS : (w + 1) * ROWS] = acc[:, :TB]
-            S[i, (w + 1) * ROWS : (w + 2) * ROWS] = acc[:, TB:]
+        w = 0 if early else 2
+        acc = product(hidden, G2, 1, CB // 2, pair + odd * 5 + w, 2).astype(BF16)
+        S[i, w * ROWS : (w + 1) * ROWS] = acc[:, :TB]
+        S[i, (w + 1) * ROWS : (w + 2) * ROWS] = acc[:, TB:]
+        if early:
+            return carry
         acc = product(hidden, G2, 1, CB // 2, pair + 4, 1)
         top, low = acc[: ROWS // 2], acc[ROWS // 2 :]
         left = lax.broadcasted_iota(jnp.int32, (ROWS // 2, TB), 1) < TB // 2
@@ -291,39 +318,97 @@
         S[i, 4 * ROWS :] = half.astype(BF16)
         return carry
 
-    H = SR // 2
-
-    def ring(step):
-        for h in (0, 1):
-            for d in (0, 1):
-                at = S.at[2 * step + d, pl.ds(h * H, H)]
-                if step:
-                    old = R.at[d, step - 1, pl.ds(h * H, H)]
-                    got(old, rS, rX.at[d, step - 1, h], xdev[1 - d])
-                    at[...] = (at[...].astype(F32) + old[...].astype(F32)).astype(BF16)
-                send(at, R.at[d, step, pl.ds(h * H, H)], rS, rX.at[d, step, h], xdev[d])
-
-    lax.fori_loop(0, 2, fc2, 0)
-    ring(0)
-    lax.fori_loop(2, 6, fc2, 0)
-    ring(1)
-    lax.fori_loop(6, 8, fc2, 0)
-    ring(2)
+    H = (SR - SB) // 2
+    B = SB // 2
+
+    def off_at(d, step):
+        return (3 - step) if d == 0 else (1 + step) % 4
+
+    def late_rows(h):
+        return pl.ds(SB + h * H, H), pl.ds(h * H, H)
+
+    def ring(step, h):
+        for d in (0, 1):
+            rows, slot = late_rows(h)
+            at = S.at[2 * off_at(d, step) + d, rows]
+            if step:
+                old = R.at[d, step - 1, slot]
+                got(old, rS, rX.at[d, step - 1, h], xdev[1 - d])
+                at[...] = (at[...].astype(F32) + old[...].astype(F32)).astype(BF16)
+            send(at, R.at[d, step, slot], rS, rX.at[d, step, h], xdev[d])
+
+    def give(off):
+        send(S.at[2 * off + 1 - yh, pl.ds(0, SB)], YB.at[off], rS, rB.at[off], hdev)
+
+    def taken(off):
+        got(YB.at[off], rS, rB.at[off], hdev)
+
+    def ring_b(step, d):
+        off, rows = jnp.where(d == 0, 3 - step, 1 + step), pl.ds(pl.multiple_of(d * B, B), B)
+        at = S.at[2 * off + yh, rows]
+        new = at[...].astype(F32) + YB[off, rows].astype(F32)
+        if step:
+            got(Q.at[d, step - 1], rS, rQ.at[d, step - 1], xdev[0])
+            new = new + Q[d, step - 1].astype(F32)
+        at[...] = new.astype(BF16)
+        send(at, Q.at[d, step], rS, rQ.at[d, step], {"ffn": yh * 4 + (x + 1 + 2 * d) % 4})
+
+    def late(first):
+        lax.fori_loop(first, first + 2, functools.partial(fc2, False), 0)
+
+    def early(first):
+        lax.fori_loop(first, first + 2, functools.partial(fc2, True), 0)
+
     o = 1 - yh
+    late(0)
+    ring(0, 0)
+    ring(0, 1)
+    early(0)
+    give(1 + 2 * yh)
+    early(2)
+    give(3 - 2 * yh)
+    late(4)
+    ring(1, 0)
+    ring(1, 1)
+    early(4)
+    give(2)
+    taken(3 - 2 * yh)
+    ring_b(0, yh)
+    late(2)
+    ring(2, 0)
+    early(6)
+    give(0)
+    taken(1 + 2 * yh)
+    ring_b(0, o)
+    ring(2, 1)
+    late(6)
+    taken(2)
+    ring_b(1, yh)
+    ring_b(1, o)
     for h in (0, 1):
-        rows = pl.ds(h * H, H)
-        at, old = S.at[6 + o, rows], R.at[o, 2, rows]
+        rows, slot = late_rows(h)
+        at, old = S.at[o, rows], R.at[o, 2, slot]
         got(old, rS, rX.at[o, 2, h], xdev[0])
         at[...] = (at[...].astype(F32) + old[...].astype(F32)).astype(BF16)
-        send(at, RY.at[rows], rS, rY.at[h], hdev)
+        send(at, RY.at[slot], rS, rY.at[h], hdev)
+    ring_b(2, yh)
+    ring_b(2, o)
+    taken(0)
     lo = pl.multiple_of((f // 2 * 9 + f % 2 * 4) * TB, TB)
     for h in (0, 1):
-        rows = pl.ds(h * H, H)
-        got(R.at[yh, 2, rows], rS, rX.at[yh, 2, h], xdev[0])
-        got(RY.at[rows], rS, rY.at[h], hdev)
-    total = S[6 + yh].astype(F32) + R[yh, 2].astype(F32) + RY[...].astype(F32)
-    main = [total[w * ROWS : (w + 1) * ROWS] for w in range(4)]
-    half = total[4 * ROWS :]
+        rows, slot = late_rows(h)
+        got(R.at[yh, 2, slot], rS, rX.at[yh, 2, h], xdev[0])
+    late = S[yh, SB:].astype(F32) + R[yh, 2].astype(F32)
+    early = S[yh, :SB].astype(F32) + YB[0].astype(F32)
+    for d in (0, 1):
+        got(Q.at[d, 2], rS, rQ.at[d, 2], xdev[1 - d])
+    for h in (0, 1):
+        rows, slot = late_rows(h)
+        got(RY.at[slot], rS, rY.at[h], hdev)
+    late = late + RY[...].astype(F32)
+    main = [early[d * B : (d + 1) * B] + Q[d, 2].astype(F32) for d in (0, 1)]
+    main += [late[w * ROWS : (w + 1) * ROWS] for w in (0, 1)]
+    half = late[2 * ROWS :]
     turned = pltpu.roll(half, TB // 2, 1)
 
     @pl.when(f % 2 == 0)
@@ -362,7 +447,7 @@
     return pl.pallas_call(
         kernel,
         out_shape=jax.ShapeDtypeStruct((ROWS, 576), BF16),
-        in_specs=[hb, vm, vm, vm, vm, hb, hb, sm, sm, sm, sm],
+        in_specs=[hb, vm, vm, vm, vm, hb, hb, sm, hb, sm, hb],
         out_specs=vm,
         scratch_shapes=[
             V((TOT + 1, TB, TB), BF16),
@@ -374,15 +459,19 @@
             V((ROWS, D), BF16),
             V((ROWS, FFS), BF16),
             V((8, SR, TB), BF16),
-            V((2, 3, SR, TB), BF16),
-            V((SR, TB), BF16),
+            V((2, 3, SR - SB, TB), BF16),
+            V((SR - SB, TB), BF16),
+            V((4, SB, TB), BF16),
+            V((2, 3, SB // 2, TB), BF16),
             V((SLOTS, 32, TB), jnp.int32),
-            dma((5,)),
+            pltpu.SMEM((1, 1), jnp.int32),
+            pltpu.SMEM((1, 1), jnp.int32),
+            dma((7,)),
             dma((2,)),
             dma((2, 2, 4, 2)),
             dma((2, 2, 4, 2)),
             dma((2,)),
-            dma((2, 8)),
+            dma((2, 9)),
             dma((2,)),
             dma,
             dma,
@@ -391,6 +480,8 @@
             dma,
             dma((2, 3, 2)),
             dma((2,)),
+            dma((4,)),
+            dma((2, 3)),
         ],
         compiler_params=pltpu.CompilerParams(
             collective_id=0, has_side_effects=True, vmem_limit_bytes=60 * 1024 * 1024

time: 140 us -> 131 us (0.936); the launches traced: 138 us -> 131 us
  Pallas kernels: 135 us -> 128 us
    pallas_call x1, Pallas kernels: 135 us -> 128 us  [on_device(): pl.pallas_call(kernel, out_shape=jax.ShapeDtypeStruct((ROWS, 576), BF16),...]
where the time goes in v3:
time: 131 us
  Pallas kernels  128 us (98%)
  local copies, waits for them, and re-layouts  1.84 us (1%)
    pallas_call x1, Pallas kernels, on_device(): pl.pallas_call(kernel, out_shape=jax.ShapeDtypeStruct((ROWS, 576), BF16),...  128 us

profile of v3, /device:TPU:2, one launch (start us, length us, event | category | flops | bytes accessed | tf_op | source)
XLA Modules:
  0.0 131.1 jit_solution(3920760804357652701)
XLA Ops:
  1.3 128.0 %shard_map.109 = bf16[256,576]{1,0:T(8,128)(2,1)} custom-call(bf16[256,4608]{1,0:T(8,128)(2,1)} %tok_h.1, f32[4608]{0:T(1024)} %gain.1, f32[4608]{0:T(1024)} %beta.1, f32[2304]{0:T(1024)} %b1.1, f32[576]{0:T(1024)} %b2.1, bf16[12,128,128]{2,1,0:T(8,128)(2,1)} %bitcast.2, bf16[12,128,128]{2,1,0:T(8,128)(2,1)} %bitcast.3, s32[1,1,12]{2,1,0:T(1,128)} %i1.1, ...), custom_call_target="tpu_custom_call" | custom-call | tf_op jit(solution)/shard_map/pallas_call | solution.py:447
  129.3 1.8 %copy.12 = bf16[256,576]{0,1:T(8,128)(2,1)} copy(bf16[256,576]{1,0:T(8,128)(2,1)} %shard_map.109) | data formatting | bytes 589824 | tf_op jit(solution)/shard_map/pallas_call | solution.py:447

commit v4 on v3

--- a/solution.py
+++ b/solution.py
@@ -14,7 +14,6 @@
 FAR = (2, 3)
 ROWS, D, FFS = 256, 4608, 2304
 RB, CB = 36, 18
-SW = 640
 SR = 1152
 SB = 512
 TOT = 32 * SLOTS
@@ -23,7 +22,7 @@
 
 def kernel(
     tok_h, gain, beta, b1, b2, t1, t2, i1, c1, i2, c2, out,
-    G1, G2, M, Tv, Ts, tok, normed, hidden, S, R, RY, YB, Q, W, n1, n2,
+    G1, G2, M, Tv, Ts, tok, normed, hidden, S, R, RY, YB, Q, W,
     ls, ss, zA, zQ, yQ, yP, dS, mS, mY, mD, mZ, rS, rX, rY, rB, rQ,
 ):
     b = lax.axis_index("blk")
@@ -38,21 +37,17 @@
     hdev = {"ffn": (1 - yh) * 4 + x}
 
     bar = pltpu.get_barrier_semaphore()
-    for dev in (*zdev, ydev, ddev, *xdev, hdev):
+    for dev in (hdev, *xdev, *zdev, ydev, ddev):
         pl.semaphore_signal(bar, inc=1, device_id=dev, device_id_type=MESH)
     tok_cp = pltpu.make_async_copy(tok_h, tok, ls.at[2])
     tok_cp.start()
-    counts = [pltpu.make_async_copy(h, num, ls.at[5 + k]) for k, (h, num) in enumerate(((c1, n1), (c2, n2)))]
-    for cp in counts:
-        cp.start()
     sub = lax.broadcasted_iota(jnp.int32, (8, TB), 0)
     lane8 = lax.broadcasted_iota(jnp.int32, (8, TB), 1)
     seen = jnp.full((8, TB), -1, jnp.int32)
-    for cp in counts:
-        cp.wait()
-    for q, (idx, num) in enumerate(((i1, n1), (i2, n2))):
+    for q, (idx, num) in enumerate(((i1, c1), (i2, c2))):
+        live = lane8 < jnp.broadcast_to(num[...], (8, TB))
         for s in range(SLOTS):
-            here = (sub == q) & (lane8 == s) & (s < num[0, 0])
+            here = (sub == q) & (lane8 == s) & live
             seen = jnp.where(here, idx[0, 0, s], seen)
     M[z * 4 + c * 2 + j] = seen
     pl.semaphore_wait(bar, 7)
@@ -194,24 +189,30 @@
         normed[rows, :] = (t * gain[...][None] + beta[...][None]).astype(BF16)
         return carry
 
-    lax.fori_loop(0, ROWS // 16, norm_rows, 0)
+    def norm_quarter(k):
+        lax.fori_loop(4 * k, 4 * k + 4, norm_rows, 0)
+
     zero_tile = jnp.zeros((TB, TB), BF16)
     G1[TOT] = zero_tile
     G2[TOT] = zero_tile
 
+    norm_quarter(0)
     y_q(0)
     a_step(0, 1)
     q_own(0)
     meta_relay(1)
+    norm_quarter(1)
     y_p(0, 0, 0)
     a_step(0, 2)
     meta_relay(2)
+    norm_quarter(2)
     q_step(0, 1)
     y_p(0, 0, 1)
     y_p(0, 1, 1)
     a_step(0, 3)
     start_y(1)
     meta_relay(3)
+    norm_quarter(3)
     q_step(0, 2)
     y_p(0, 0, 2)
     y_p(0, 1, 2)
@@ -295,6 +296,12 @@
     pltpu.make_async_copy(t2, G2.at[pl.ds(own, SLOTS)], ls.at[1]).wait()
     arrived(1, base(1 - c, 0, 0), TOT // 2, dS.at[1], ddev)
 
+    def half_block(v, odd):
+        top, low = v[: ROWS // 2], v[ROWS // 2 :]
+        left = lax.broadcasted_iota(jnp.int32, (ROWS // 2, TB), 1) < TB // 2
+        turned = pltpu.roll(jnp.where(odd == 1, top, low), TB // 2, 1)
+        return jnp.where(left == (odd == 1), turned, jnp.where(odd == 1, low, top))
+
     def fc2(early, i, carry):
         order = ((3, 0), (1, 1), (1, 0), (3, 1), (2, 0), (2, 1), (0, 0), (0, 1))
         off, d = jnp.int32(0), i % 2
@@ -311,11 +318,7 @@
         if early:
             return carry
         acc = product(hidden, G2, 1, CB // 2, pair + 4, 1)
-        top, low = acc[: ROWS // 2], acc[ROWS // 2 :]
-        left = lax.broadcasted_iota(jnp.int32, (ROWS // 2, TB), 1) < TB // 2
-        turned = pltpu.roll(jnp.where(odd == 1, top, low), TB // 2, 1)
-        half = jnp.where(left == (odd == 1), turned, jnp.where(odd == 1, low, top))
-        S[i, 4 * ROWS :] = half.astype(BF16)
+        S[i, 4 * ROWS :] = half_block(acc, odd).astype(BF16)
         return carry
 
     H = (SR - SB) // 2
@@ -394,34 +397,45 @@
     ring_b(2, yh)
     ring_b(2, o)
     taken(0)
-    lo = pl.multiple_of((f // 2 * 9 + f % 2 * 4) * TB, TB)
+    first = f // 2 * 9
+
+    def residual(w):
+        if w < 4:
+            return tok[:, pl.ds(pl.multiple_of((first + f % 2 * 5 + w) * TB, TB), TB)].astype(F32)
+        return half_block(tok[:, pl.ds(pl.multiple_of((first + 4) * TB, TB), TB)].astype(F32), f % 2)
+
+    def finish(sums, at, shared):
+        e = b2[...][None]
+        for w, v in sums.items():
+            if w < 4:
+                out[at + w * TB : at + (w + 1) * TB, :] = (v + e[:, at + w * TB : at + (w + 1) * TB]).astype(BF16).T
+            else:
+                twice = jnp.concatenate([e[:, shared : shared + TB // 2]] * 2, axis=1)
+                v = (v + twice).astype(BF16).T
+                out[shared : shared + TB // 2, : ROWS // 2] = v[: TB // 2]
+                out[shared : shared + TB // 2, ROWS // 2 :] = v[TB // 2 :]
+
+    def finish_either(sums):
+        pl.when(f % 2 == 0)(lambda: finish(sums, 0, 4 * TB))
+        pl.when(f % 2 == 1)(lambda: finish(sums, TB // 2, 0))
+
     for h in (0, 1):
         rows, slot = late_rows(h)
         got(R.at[yh, 2, slot], rS, rX.at[yh, 2, h], xdev[0])
-    late = S[yh, SB:].astype(F32) + R[yh, 2].astype(F32)
-    early = S[yh, :SB].astype(F32) + YB[0].astype(F32)
+        got(RY.at[slot], rS, rY.at[h], hdev)
+    sums = {}
+    for w in (2, 3, 4):
+        n = ROWS if w < 4 else ROWS // 2
+        rows, slot = pl.ds(w * ROWS, n), pl.ds(w * ROWS - SB, n)
+        sums[w] = S[yh, rows].astype(F32) + R[yh, 2, slot].astype(F32) + RY[slot].astype(F32) + residual(w)
+    finish_either(sums)
     for d in (0, 1):
         got(Q.at[d, 2], rS, rQ.at[d, 2], xdev[1 - d])
-    for h in (0, 1):
-        rows, slot = late_rows(h)
-        got(RY.at[slot], rS, rY.at[h], hdev)
-    late = late + RY[...].astype(F32)
-    main = [early[d * B : (d + 1) * B] + Q[d, 2].astype(F32) for d in (0, 1)]
-    main += [late[w * ROWS : (w + 1) * ROWS] for w in (0, 1)]
-    half = late[2 * ROWS :]
-    turned = pltpu.roll(half, TB // 2, 1)
-
-    @pl.when(f % 2 == 0)
-    def _():
-        full = jnp.concatenate(main + [jnp.concatenate([half, turned], axis=0)], axis=1)
-        full = full + tok[:, pl.ds(lo, SW)].astype(F32)
-        out[...] = (full[:, :576] + b2[...][None]).astype(BF16)
-
-    @pl.when(f % 2 == 1)
-    def _():
-        full = jnp.concatenate([jnp.concatenate([turned, half], axis=0)] + main, axis=1)
-        full = full + tok[:, pl.ds(lo, SW)].astype(F32)
-        out[...] = (full[:, SW - 576 :] + b2[...][None]).astype(BF16)
+    sums = {}
+    for w in (0, 1):
+        rows = pl.ds(w * ROWS, ROWS)
+        sums[w] = S[yh, rows].astype(F32) + YB[0, rows].astype(F32) + Q[w, 2].astype(F32) + residual(w)
+    finish_either(sums)
 
     for q in (0, 1):
         all_sent = G[q].at[pl.ds(0, 372)]
@@ -446,8 +460,8 @@
     dma, V = pltpu.SemaphoreType.DMA, pltpu.VMEM
     return pl.pallas_call(
         kernel,
-        out_shape=jax.ShapeDtypeStruct((ROWS, 576), BF16),
-        in_specs=[hb, vm, vm, vm, vm, hb, hb, sm, hb, sm, hb],
+        out_shape=jax.ShapeDtypeStruct((576, ROWS), BF16),
+        in_specs=[hb, vm, vm, vm, vm, hb, hb, sm, vm, sm, vm],
         out_specs=vm,
         scratch_shapes=[
             V((TOT + 1, TB, TB), BF16),
@@ -464,9 +478,7 @@
             V((4, SB, TB), BF16),
             V((2, 3, SB // 2, TB), BF16),
             V((SLOTS, 32, TB), jnp.int32),
-            pltpu.SMEM((1, 1), jnp.int32),
-            pltpu.SMEM((1, 1), jnp.int32),
-            dma((7,)),
+            dma((5,)),
             dma((2,)),
             dma((2, 2, 4, 2)),
             dma((2, 2, 4, 2)),
@@ -488,7 +500,7 @@
         ),
     )(
         tokens, gain, beta, b1, b2, t1.reshape(SLOTS, TB, TB), t2.reshape(SLOTS, TB, TB), i1, n1, i2, n2,
-    )
+    ).T
 
 
 def solution(mesh):

time: 131 us -> 130 us (level)
    pallas_call x1 -> x0, local copies, waits for them, and re-layouts: 1.84 us -> none  [on_device(): pl.pallas_call(kernel, out_shape=jax.ShapeDtypeStruct((ROWS, 576), BF16),...]
    unnamed x0 -> x1, local copies, waits for them, and re-layouts: none -> 1.69 us
    pallas_call x1, Pallas kernels: 128 us -> 127 us  [on_device(): pl.pallas_call(kernel, out_shape=jax.ShapeDtypeStruct((576, ROWS), BF16),...]
where the time goes in v4:
time: 130 us
  Pallas kernels  127 us (98%)
  local copies, waits for them, and re-layouts  1.69 us (1%)
  between operations  1.3 us (1%)
    pallas_call x1, Pallas kernels, on_device(): pl.pallas_call(kernel, out_shape=jax.ShapeDtypeStruct((576, ROWS), BF16),...  127 us

profile of v4, /device:TPU:2, one launch (start us, length us, event | category | flops | bytes accessed | tf_op | source)
XLA Modules:
  0.0 129.7 jit_solution(11719898789303320066)
XLA Ops:
  1.3 126.7 %shard_map.109 = bf16[576,256]{1,0:T(8,128)(2,1)} custom-call(bf16[256,4608]{1,0:T(8,128)(2,1)} %tok_h.1, f32[4608]{0:T(1024)} %gain.1, f32[4608]{0:T(1024)} %beta.1, f32[2304]{0:T(1024)} %b1.1, f32[576]{0:T(1024)} %b2.1, bf16[12,128,128]{2,1,0:T(8,128)(2,1)} %bitcast.4, bf16[12,128,128]{2,1,0:T(8,128)(2,1)} %bitcast.5, s32[1,1,12]{2,1,0:T(1,128)} %i1.1, ...), custom_call_target="tpu_custom_call" | custom-call | tf_op jit(solution)/shard_map/pallas_call | solution.py:461
  128.0 1.7 %copy.15 = bf16[256,576]{0,1:T(8,128)(2,1)} copy(bf16[256,576]{0,1:T(8,128)(2,1)} %bitcast.3) | data formatting | bytes 589824
